TPU v7x, 512 devices: a whole 4x4x16 slice. The times are simulated.
512 devices in a mesh: replica: 4 (over z_hi, core), inner: 128 (over z_lo, x, y).
Axes of the slice: x: 4, y: 4, z: 16 (z_hi: 2, z_lo: 8; z = z_hi * 8 + z_lo), core: 2. Of those that a mesh axis runs over, the one named last changes fastest.
Arguments:
- square_weights: float32 [2, 1024, 1024], P(None, 'inner'), may hold values from -6 to 6
- square_copies: float32 [4, 2, 1024, 1024], P('replica', None, 'inner'), may hold values from -6 to 6
- square_moment: float32 [2, 1024, 1024], P(None, 'inner'), may hold values from -6 to 6
- broad_weights: float32 [2, 1024, 2048], P(None, 'inner'), may hold values from -6 to 6
- broad_copies: float32 [4, 2, 1024, 2048], P('replica', None, 'inner'), may hold values from -6 to 6
- broad_moment: float32 [2, 1024, 2048], P(None, 'inner'), may hold values from -6 to 6
- embed_weights: float32 [16384, 1024], P('inner'), may hold values from -6 to 6
- embed_copies: float32 [4, 16384, 1024], P('replica', 'inner'), may hold values from -90 to 90, as said below
- embed_moment: float32 [16384, 1024], P('inner'), may hold values from -6 to 6
- embed_error: float32 [4, 16384, 1024], P('replica', 'inner'), may hold values from -3 to 3
- warm_start: float32 [64, 1024], replicated, may hold values from -6 to 6
Outputs:
- square_updated: float32 [2, 1024, 1024], P(None, 'inner')
- square_velocity: float32 [2, 1024, 1024], P(None, 'inner')
- broad_updated: float32 [2, 1024, 2048], P(None, 'inner')
- broad_velocity: float32 [2, 1024, 2048], P(None, 'inner')
- embed_updated: float32 [16384, 1024], P('inner')
- embed_velocity: float32 [16384, 1024], P('inner')
- embed_carried: float32 [4, 16384, 1024], P('replica', 'inner')
Inputs may be any that keep to these rules, and one draw needn't show every extreme that they name: `embed_copies`: each replica's embedding after its inner steps.
All inputs are finite; a program needn't handle non-finite values.
Results may differ from a plain program's by a relative error of at most 0.0001.
Values sent between devices are 32-bit elements; how exact they have to be, the bound alone decides.
A program may use at most 64 MiB of HBM per device.

v0:
```python
import jax
import jax.numpy as jnp
from jax import lax
from jax.sharding import PartitionSpec as P

outer_rate = 0.7
momentum_decay = 0.9


def nesterov(weights, gradient, moment):
    velocity = momentum_decay * moment + gradient
    return (weights - outer_rate * (gradient + momentum_decay * velocity), velocity)


def local(
    square_weights,
    square_copies,
    square_moment,
    broad_weights,
    broad_copies,
    broad_moment,
    embed_weights,
    embed_copies,
    embed_moment,
    embed_error,
    warm_start,
):
    replicas = lax.axis_size("replica")
    highest = lax.Precision.HIGHEST
    contract_last = (((1,), (1,)), ((), ()))
    square_term = square_weights - square_copies[0]
    broad_term = broad_weights - broad_copies[0]
    corrected = embed_weights - embed_copies[0] + embed_error[0]
    square_sum, broad_sum = lax.psum((square_term, broad_term), "replica")
    left_local = lax.dot_general(warm_start, corrected, contract_last, precision=highest)
    left_factor = lax.psum(left_local, "replica") / replicas
    gram_local = lax.dot_general(left_factor, left_factor, contract_last, precision=highest)
    gram_matrix = lax.psum(gram_local, "inner")
    lower_factor = jnp.linalg.cholesky(gram_matrix)
    basis_rows = lax.linalg.triangular_solve(lower_factor, left_factor, left_side=True, lower=True)
    right_term = jnp.dot(basis_rows, corrected, precision=highest)
    right_total = lax.psum(right_term, ("replica", "inner"))
    right_factor = right_total / replicas
    embed_step = lax.dot_general(
        basis_rows, right_factor, (((0,), (0,)), ((), ())), precision=highest
    )
    embed_updated, embed_velocity = nesterov(embed_weights, embed_step, embed_moment)
    square_updated, square_velocity = nesterov(square_weights, square_sum / replicas, square_moment)
    broad_updated, broad_velocity = nesterov(broad_weights, broad_sum / replicas, broad_moment)
    embed_carried = (corrected - embed_step)[None]
    return (
        square_updated,
        square_velocity,
        broad_updated,
        broad_velocity,
        embed_updated,
        embed_velocity,
        embed_carried,
    )


def solution(mesh):
    in_specs = (
        P(None, "inner", None),
        P("replica", None, "inner", None),
        P(None, "inner", None),
        P(None, "inner", None),
        P("replica", None, "inner", None),
        P(None, "inner", None),
        P("inner", None),
        P("replica", "inner", None),
        P("inner", None),
        P("replica", "inner", None),
        P(),
    )
    out_specs = (
        P(None, "inner", None),
        P(None, "inner", None),
        P(None, "inner", None),
        P(None, "inner", None),
        P("inner", None),
        P("inner", None),
        P("replica", "inner", None),
    )
    return jax.shard_map(local, mesh=mesh, in_specs=in_specs, out_specs=out_specs, check_vma=False)
```

profile of v0, /device:TPU:1, one launch (start us, length us, event | category | flops | bytes accessed | tf_op | source)
XLA Modules:
  0.0 1638.2 jit_solution(11594696563197630290)
XLA Ops:
  7.2 0.0 copy-start
  7.2 0.0 all-reduce.4.cloned.1.call-start
  7.2 1.5 bitcast_add_fusion
  8.7 0.0 copy-done
  8.7 0.7 convolution_bitcast_fusion
  9.4 33.8 %psum.37 = f32[64,128]{1,0:T(8,128)S(1)} all-reduce(f32[64,128]{1,0:T(8,128)S(1)} %convolution_bitcast_fusion), channel_id=1, replica_groups=mesh['replica'=4,'inner'=128] {'replica'}, use_global_device_ids=true, to_apply=%region_2.0 | all-reduce | flops 8192 | bytes 65536 | tf_op jit(solution)/shard_map/psum | solution.py:36
  43.2 0.2 fusion.8
  43.4 926.7 %psum.38 = f32[64,64]{0,1:T(8,128)S(1)} all-reduce(f32[64,64]{0,1:T(8,128)S(1)} %fusion.8), channel_id=1, replica_groups=mesh['replica'=4,'inner'=128] {'inner'}, use_global_device_ids=true, to_apply=%region_3.0 | all-reduce | flops 4096 | bytes 32768 | tf_op jit(solution)/shard_map/psum | solution.py:38
  970.1 0.1 copy.19
  970.2 5.8 cholesky.16
  976.1 0.6 compare_reduce_fusion
  976.7 0.7 fusion.3
  977.4 4.9 custom-call.6
  982.3 0.3 fusion.4
  982.5 0.0 copy-start.2
  982.5 0.0 copy-start.5
  982.6 0.0 copy-start.4
  982.6 0.0 copy-start.7
  982.6 1.1 fusion.17
  983.7 0.0 copy-start.1
  983.7 0.0 copy-start.3
  983.7 0.0 all-reduce.4.cloned.1.call-update
  983.8 0.0 all-reduce.6.cloned.1.call-start
  983.8 0.0 copy-done.2
  983.8 0.0 copy-done.5
  983.8 0.7 bitcast_subtract_fusion.1
  984.5 0.0 copy-done.4
  984.5 0.0 copy-done.7
  984.5 0.6 bitcast_subtract_fusion.2
  985.1 0.0 all-reduce.6.cloned.1.call-update
  985.2 0.0 copy-start.6
  985.2 561.2 %all-reduce.4.cloned.1.call-done = f32[64,1024]{1,0:T(8,128)} async-done(((f32[64,1024]{1,0:T(8,128)}), f32[64,1024]{1,0:T(8,128)}) %all-reduce.4.cloned.1.call-update) | async-done | bytes 262160 | tf_op jit(solution)/shard_map/psum | solution.py:42
  1546.4 0.0 copy-done.1
  1546.4 0.0 copy-done.3
  1546.4 2.8 multiply_subtract_fusion
  1549.2 79.8 %all-reduce.6.cloned.1.call-done = (f32[2,8,1024]{2,1,0:T(8,128)}, f32[2,8,2048]{2,1,0:T(8,128)}) async-done(((f32[2,8,1024]{2,1,0:T(8,128)}, f32[2,8,2048]{2,1,0:T(8,128)}), (f32[2,8,1024]{2,1,0:T(8,128)}, f32[2,8,2048]{2,1,0:T(8,128)})) %all-reduce.6.cloned.1.call-update) | async-done | bytes 196624 | tf_op jit(solution)/shard_map/psum | solution.py:34
  1629.1 0.0 copy-done.6
  1629.1 0.0 copy-start.8
  1629.1 0.0 copy-start.9
  1629.1 1.7 multiply_subtract_fusion.1
  1630.7 0.0 copy-done.8
  1630.7 0.0 copy-done.9
  1630.7 0.7 multiply_subtract_fusion.2
  (2 shorter events, 0.0 us)
Async XLA Ops:
  7.2 1.6 copy-start
  7.2 1539.2 %all-reduce.4.cloned.1.call-start = ((), (), s32[]{:S(2)}) async-start(), calls=%async_computation | async-start | bytes 524288 | tf_op jit(solution)/shard_map/psum | solution.py:42
  982.5 1.3 copy-start.2
  982.5 1.3 copy-start.5
  982.6 1.9 copy-start.4
  982.6 1.9 copy-start.7
  983.7 562.7 %copy-start.1 = (f32[128,1024]{1,0:T(8,128)S(1)}, f32[128,1024]{1,0:T(8,128)}, u32[]{:S(2)}) copy-start(f32[128,1024]{1,0:T(8,128)} %param.17) | copy-start | bytes 1572868
  983.7 562.7 %copy-start.3 = (f32[128,1024]{1,0:T(8,128)S(1)}, f32[128,1024]{1,0:T(8,128)}, u32[]{:S(2)}) copy-start(f32[128,1024]{1,0:T(8,128)} %param.19) | copy-start | bytes 1572868
  983.8 645.3 %all-reduce.6.cloned.1.call-start = ((), (), s32[]{:S(2)}) async-start(), calls=%async_computation.1 | async-start | bytes 393216 | tf_op jit(solution)/shard_map/psum | solution.py:34
  985.2 643.9 %copy-start.6 = (f32[2,8,2048]{2,1,0:T(8,128)S(1)}, f32[2,8,2048]{2,1,0:T(8,128)}, u32[]{:S(2)}) copy-start(f32[2,8,2048]{2,1,0:T(8,128)} %param.16) | copy-start | bytes 393220
  1629.1 1.7 copy-start.8
  1629.1 1.7 copy-start.9
Sparse Core Ops, SparseCore 0:
  983.9 562.4 all-reduce.3
  1550.2 78.7 all-reduce.5
where the time goes:
time: 1640 us
  blocking collectives  961 us (59%)
  waiting for transfers between devices  641 us (39%)
  other arithmetic  17.2 us (1%)
    psum x1, blocking collectives, local(): gram_matrix = lax.psum(gram_local, 'inner')  927 us
    psum x1, waiting for transfers between devices, local(): right_total = lax.psum(right_term, ('replica', 'inner'))  561 us
    psum x1, waiting for transfers between devices, local(): square_sum, broad_sum = lax.psum((square_term, broad_term), 'replica')  79.8 us
    psum x1, blocking collectives, local(): left_factor = lax.psum(left_local, 'replica') / replicas  33.8 us
  transfers between devices with their start and end apart: 2, of which 2 were waited for; matrix products, arithmetic and copies ran while one was open for 0% of the time, Pallas kernels for 0%

commit v1 on v0

v1 whole, which is shorter than its diff:
```python
import jax
import jax.numpy as jnp
from jax import lax
from jax.experimental import pallas as pl
from jax.experimental.pallas import tpu as pltpu
from jax.sharding import PartitionSpec as P

outer_rate = 0.7
momentum_decay = 0.9
MESH = pl.DeviceIdType.MESH
HIGHEST = lax.Precision.HIGHEST
PLANE = sorted(((dx, dy) for dx in range(4) for dy in range(4) if dx or dy), key=lambda d: -(min(d[0], 4 - d[0]) + min(d[1], 4 - d[1])))
RING = sorted(range(1, 16), key=lambda d: -min(d, 16 - d))


def dot(a, b):
    return jnp.dot(a, b, precision=HIGHEST, preferred_element_type=jnp.float32)


def dot_t(a, b):
    return lax.dot_general(a, b, (((1,), (1,)), ((), ())), precision=HIGHEST, preferred_element_type=jnp.float32)


def sub(v, j):
    return jnp.broadcast_to(v[j : j + 1, :], v.shape)


def lower_inverse(a):
    rows = lax.broadcasted_iota(jnp.int32, (8, 128), 0)
    scale = []
    for kb in range(8):
        cols = {}
        for j in range(8):
            lane = 64 + 8 * kb + j
            for b in range(kb, 8):
                cols[b, j] = jnp.broadcast_to(a[b][:, lane : lane + 1], (8, 128))
        inv_pivots = jnp.ones((8, 128), jnp.float32)
        for j in range(8):
            inv = 1.0 / sub(cols[kb, j], j)
            inv_pivots = jnp.where(rows == j, inv, inv_pivots)
            row = sub(a[kb], j)
            later = [sub(cols[kb, i], j) for i in range(j + 1, 8)]
            for b in range(kb, 8):
                factor = cols[b, j] * inv
                if b == kb:
                    factor = jnp.where(rows > j, factor, 0.0)
                a[b] = a[b] - factor * row
                for i in range(j + 1, 8):
                    cols[b, i] = cols[b, i] - factor * later[i - j - 1]
        scale.append(jnp.sqrt(inv_pivots))
    return [a[b] * scale[b] for b in range(8)]


def comm_kernel(
    sqw, sqc, brw, brc, ew, ec, ee, ws,
    sq_out, br_out, h_out, p_out,
    vsqw, vsqc, vbrw, vbrc, vew, vec, vee, vws,
    corr, corr_in, l_part, l_core, l_send, l_z, l_full, term, t_core, t_send, t_z, t_full,
    h_part, h_in, h_zs, h_z, h_full, g_part, g_in, g_zs, g_z, g_full,
    load_sem, one_send, one_recv, rs_send, rs_recv, grs_send, grs_recv, z_send, z_recv, gz_send, gz_recv,
    ag_send, ag_recv, gag_send, gag_recv, fw_send, fw_recv,
):
    rep, inn = lax.axis_index("replica"), lax.axis_index("inner")
    core, zhi = lax.rem(rep, 2), lax.div(rep, 2)
    zlo, x, y = lax.div(inn, 16), lax.rem(lax.div(inn, 4), 4), lax.rem(inn, 4)
    z, me = zhi * 8 + zlo, x * 4 + y
    other = 1 - core

    loads = []
    for i, (src, dst) in enumerate(((ew, vew), (ec, vec), (ee, vee), (ws, vws), (sqw, vsqw), (sqc, vsqc), (brw, vbrw), (brc, vbrc))):
        copy = pltpu.make_async_copy(src, dst, load_sem.at[i])
        copy.start()
        loads.append(copy)

    def plane(dx, dy):
        return lax.rem(x + dx, 4) * 4 + lax.rem(y + dy, 4)

    def at_z(d):
        return lax.rem(z + d, 16)

    def dev(c, zz, q):
        return (lax.div(zz, 8) * 2 + c, lax.rem(zz, 8) * 16 + q)

    partners = [dev(other, z, me)]
    for dx, dy in PLANE:
        partners += [dev(core, z, plane(dx, dy)), dev(other, z, plane(dx, dy))]
    for d in RING:
        partners.append(dev(core, at_z(d), me))
    barrier = pltpu.get_barrier_semaphore()
    for device in partners:
        pl.semaphore_signal(barrier, inc=1, device_id=device, device_id_type=MESH)

    sends = []

    def send(src, dst, ss, rs, device):
        copy = pltpu.make_async_remote_copy(src, dst, ss, rs, device_id=device, device_id_type=MESH)
        copy.start()
        sends.append(copy)
        return copy

    def arrived(dst, ss, rs):
        pltpu.make_async_remote_copy(dst, dst, ss, rs, device_id=partners[0], device_id_type=MESH).wait_recv()

    for i in range(4):
        loads[i].wait()
    corr[...] = vew[...] - vec[...] + vee[...]
    left = dot_t(vws[...], corr[...])
    l_part[0] = left[:32]
    l_part[1] = left[32:]
    pl.semaphore_wait(barrier, len(partners))
    twin = partners[0]
    send(l_part.at[other], l_core, one_send.at[0], one_recv.at[0], twin)
    send(corr, corr_in, one_send.at[1], one_recv.at[1], twin)
    for i in range(4, 8):
        loads[i].wait()
    for i in range(2):
        term[i] = vsqw[i] - vsqc[i]
        broad = vbrw[i] - vbrc[i]
        term[2 + 2 * i] = broad[:, :1024]
        term[3 + 2 * i] = broad[:, 1024:]
    send(term.at[pl.ds(3 * other, 3)], t_core, one_send.at[2], one_recv.at[2], twin)
    far = dev(core, at_z(8), me)
    arrived(l_core, one_send.at[0], one_recv.at[0])
    l_send[...] = l_part[core] + l_core[...]
    send(l_send, l_z, one_send.at[3], one_recv.at[3], far)
    arrived(t_core, one_send.at[2], one_recv.at[2])
    t_send[...] = term[pl.ds(3 * core, 3)] + t_core[...]
    send(t_send, t_z, one_send.at[4], one_recv.at[4], far)
    arrived(corr_in, one_send.at[1], one_recv.at[1])
    total = vew
    total[...] = corr[...] + corr_in[...]

    arrived(l_z, one_send.at[3], one_recv.at[3])
    mine = (l_send[...] + l_z[...]) * 0.25
    l_full[core] = mine
    send(l_full.at[core], l_full.at[core], one_send.at[5], one_recv.at[5], twin)
    for cb in range(4):
        block = dot(mine, total[:, 256 * cb : 256 * cb + 256]) * 0.25
        for rb in range(4):
            h_part[4 * rb + cb] = block[8 * rb : 8 * rb + 8]
    for i, (dx, dy) in enumerate(PLANE):
        q = plane(dx, dy)
        send(h_part.at[q], h_in.at[me], rs_send.at[i], rs_recv.at[me], dev(core, z, q))
    h_in[me] = h_part[me]

    arrived(l_full.at[other], one_send.at[5], one_recv.at[5])
    left_all = jnp.concatenate([l_full[0], l_full[1]], axis=0)
    nothing = jnp.zeros_like(left_all)
    packed = dot_t(mine[:16], jnp.concatenate([left_all, nothing], axis=0)) + dot_t(mine[16:], jnp.concatenate([nothing, left_all], axis=0))
    for i in range(16):
        g_part[i] = packed[i : i + 1]
    for i, (dx, dy) in enumerate(PLANE):
        q = plane(dx, dy)
        send(g_part.at[q], g_in.at[me], grs_send.at[i], grs_recv.at[me], dev(core, z, q))
    g_in[me] = g_part[me]

    def plane_wait(dst, ss, rs):
        for i, (dx, dy) in enumerate(PLANE):
            q = plane(dx, dy)
            arrived(dst.at[q], ss.at[i], rs.at[q])

    def added(ref, n):
        out = ref[0]
        for i in range(1, n):
            out = out + ref[i]
        return out

    plane_wait(g_in, grs_send, grs_recv)
    g_sum = added(g_in, 16)
    g_zs[...] = g_sum
    g_z[zlo] = g_sum
    for d in range(1, 8):
        peer = zhi * 8 + lax.rem(zlo + d, 8)
        send(g_zs, g_z.at[zlo], gz_send.at[d], gz_recv.at[zlo], dev(core, peer, me))
    plane_wait(h_in, rs_send, rs_recv)
    h_sum = added(h_in, 16)
    h_zs[...] = h_sum
    h_z[z] = h_sum
    for d in RING:
        send(h_zs, h_z.at[z], z_send.at[d], z_recv.at[z], dev(core, at_z(d), me))

    for d in range(1, 8):
        peer = lax.rem(zlo + d, 8)
        arrived(g_z.at[peer], gz_send.at[d], gz_recv.at[peer])
    g_full[core, me] = added(g_z, 8)
    mine_g = g_full.at[core, me]
    slot = core * 16 + me
    for i, (dx, dy) in enumerate(PLANE):
        q = plane(dx, dy)
        for k, c in enumerate((core, other)):
            send(mine_g, mine_g, gag_send.at[2 * i + k], gag_recv.at[slot], dev(c, z, q))
    send(mine_g, mine_g, gag_send.at[30], gag_recv.at[slot], twin)

    arrived(t_z, one_send.at[4], one_recv.at[4])
    t_full[pl.ds(3 * core, 3)] = (t_send[...] + t_z[...]) * 0.25
    send(t_full.at[pl.ds(3 * core, 3)], t_full.at[pl.ds(3 * core, 3)], one_send.at[6], one_recv.at[6], twin)

    for d in RING:
        peer = at_z(d)
        arrived(h_z.at[peer], z_send.at[d], z_recv.at[peer])
    h_full[core, me] = added(h_z, 16)
    mine_h = h_full.at[core, me]
    for i, (dx, dy) in enumerate(PLANE):
        send(mine_h, mine_h, ag_send.at[i], ag_recv.at[me], dev(core, z, plane(dx, dy)))
    send(mine_h, mine_h, fw_send.at[15], fw_recv.at[me], twin)

    for i, (dx, dy) in enumerate(PLANE):
        q = plane(dx, dy)
        for k, c in enumerate((core, other)):
            arrived(g_full.at[c, q], gag_send.at[2 * i + k], gag_recv.at[c * 16 + q])
    arrived(g_full.at[other, me], gag_send.at[30], gag_recv.at[other * 16 + me])

    lanes = lax.broadcasted_iota(jnp.int32, (8, 128), 1)
    rows = lax.broadcasted_iota(jnp.int32, (8, 128), 0)
    blocks = [None] * 8
    for c in range(2):
        for part in range(2):
            tile = jnp.concatenate([g_full[c, 8 * part + i] for i in range(8)], axis=0)
            blocks[4 * c + part] = pltpu.roll(tile, 64, 1)
            blocks[4 * c + 2 + part] = tile
    for b in range(8):
        blocks[b] = jnp.where(lanes >= 64, blocks[b], jnp.where(lanes == rows + 8 * b, 1.0, 0.0))
    inverse = jnp.concatenate(lower_inverse(blocks), axis=0)[:, :64]
    p_out[...] = dot(dot_t(left_all.T, inverse), inverse)

    for i, (dx, dy) in enumerate(PLANE):
        q = plane(dx, dy)
        arrived(h_full.at[core, q], ag_send.at[i], ag_recv.at[q])
        send(h_full.at[core, q], h_full.at[core, q], fw_send.at[i], fw_recv.at[q], twin)
    arrived(t_full.at[pl.ds(3 * other, 3)], one_send.at[6], one_recv.at[6])
    for i in range(2):
        sq_out[i] = t_full[i]
        br_out[i, :, :1024] = t_full[2 + 2 * i]
        br_out[i, :, 1024:] = t_full[3 + 2 * i]
    for i, (dx, dy) in enumerate(PLANE):
        q = plane(dx, dy)
        arrived(h_full.at[other, q], fw_send.at[i], fw_recv.at[q])
    arrived(h_full.at[other, me], fw_send.at[15], fw_recv.at[me])
    for c in range(2):
        for rb in range(4):
            for cb in range(4):
                h_out[32 * c + 8 * rb : 32 * c + 8 * rb + 8, 256 * cb : 256 * cb + 256] = h_full[c, 4 * rb + cb]
    for copy in sends:
        copy.wait_send()


def communicate(sqw, sqc, brw, brc, ew, ec, ee, ws):
    f32 = jnp.float32
    vmem = lambda *shape: pltpu.VMEM(shape, f32)
    dma = lambda n: pltpu.SemaphoreType.DMA((n,))
    return pl.pallas_call(
        comm_kernel,
        name="exchange",
        out_shape=(
            jax.ShapeDtypeStruct((2, 8, 1024), f32),
            jax.ShapeDtypeStruct((2, 8, 2048), f32),
            jax.ShapeDtypeStruct((64, 1024), f32),
            jax.ShapeDtypeStruct((128, 64), f32),
        ),
        in_specs=[pl.BlockSpec(memory_space=pl.ANY)] * 8,
        out_specs=tuple(pl.BlockSpec(memory_space=pltpu.VMEM) for _ in range(4)),
        scratch_shapes=[
            vmem(2, 8, 1024), vmem(2, 8, 1024), vmem(2, 8, 2048), vmem(2, 8, 2048),
            vmem(128, 1024), vmem(128, 1024), vmem(128, 1024), vmem(64, 1024),
            vmem(128, 1024), vmem(128, 1024), vmem(2, 32, 128), vmem(32, 128), vmem(32, 128), vmem(32, 128), vmem(2, 32, 128),
            vmem(6, 8, 1024), vmem(3, 8, 1024), vmem(3, 8, 1024), vmem(3, 8, 1024), vmem(6, 8, 1024),
            vmem(16, 8, 256), vmem(16, 8, 256), vmem(8, 256), vmem(16, 8, 256), vmem(2, 16, 8, 256),
            vmem(16, 1, 128), vmem(16, 1, 128), vmem(1, 128), vmem(8, 1, 128), vmem(2, 16, 1, 128),
            dma(8), dma(7), dma(7), dma(15), dma(16), dma(15), dma(16), dma(16), dma(16), dma(8), dma(8),
            dma(15), dma(16), dma(31), dma(32), dma(16), dma(16),
        ],
        compiler_params=pltpu.CompilerParams(collective_id=0, has_side_effects=True, vmem_limit_bytes=16 << 20),
    )(sqw, sqc, brw, brc, ew, ec, ee, ws)


def nesterov(weights, gradient, moment):
    velocity = momentum_decay * moment + gradient
    return (weights - outer_rate * (gradient + momentum_decay * velocity), velocity)


def update_kernel(sqs, sqw, sqm, brs, brw, brm, ew, ec, em, ee, p, h, squ, sqv, bru, brv, eu, ev, er):
    squ[...], sqv[...] = nesterov(sqw[...], sqs[...], sqm[...])
    bru[...], brv[...] = nesterov(brw[...], brs[...], brm[...])
    for cb in range(4):
        at = (slice(None), slice(256 * cb, 256 * cb + 256))
        step = dot(p[...], h[at])
        eu[at], ev[at] = nesterov(ew[at], step, em[at])
        er[at] = ew[at] - ec[at] + ee[at] - step


def local(
    square_weights,
    square_copies,
    square_moment,
    broad_weights,
    broad_copies,
    broad_moment,
    embed_weights,
    embed_copies,
    embed_moment,
    embed_error,
    warm_start,
):
    sq_sum, br_sum, h, p = communicate(
        square_weights, square_copies[0], broad_weights, broad_copies[0], embed_weights, embed_copies[0], embed_error[0], warm_start
    )
    shapes = [square_weights.shape] * 2 + [broad_weights.shape] * 2 + [embed_weights.shape] * 3
    outs = pl.pallas_call(
        update_kernel,
        name="update",
        out_shape=tuple(jax.ShapeDtypeStruct(s, jnp.float32) for s in shapes),
        compiler_params=pltpu.CompilerParams(vmem_limit_bytes=16 << 20),
    )(
        sq_sum, square_weights, square_moment, br_sum, broad_weights, broad_moment,
        embed_weights, embed_copies[0], embed_moment, embed_error[0], p, h,
    )
    return (*outs[:6], outs[6][None])


def solution(mesh):
    in_specs = (
        P(None, "inner", None),
        P("replica", None, "inner", None),
        P(None, "inner", None),
        P(None, "inner", None),
        P("replica", None, "inner", None),
        P(None, "inner", None),
        P("inner", None),
        P("replica", "inner", None),
        P("inner", None),
        P("replica", "inner", None),
        P(),
    )
    out_specs = (
        P(None, "inner", None),
        P(None, "inner", None),
        P(None, "inner", None),
        P(None, "inner", None),
        P("inner", None),
        P("inner", None),
        P("replica", "inner", None),
    )
    return jax.shard_map(local, mesh=mesh, in_specs=in_specs, out_specs=out_specs, check_vma=False)
```

time: 1640 us -> 62.5 us (0.04)
  blocking collectives: 961 us -> 0 us
  waiting for transfers between devices: 641 us -> 0 us
  Pallas kernels: 0 us -> 52.9 us
  other arithmetic: 17.2 us -> 0 us
    psum x2 -> x0, blocking collectives: 961 us -> none  [the longest x1 927 us: local(): gram_matrix = lax.psum(gram_local, 'inner')]
    psum x2 -> x0, waiting for transfers between devices: 641 us -> none  [the longest x1 561 us: local(): right_total = lax.psum(right_term, ('replica', 'inner'))]
    pallas_call x0 -> x2, Pallas kernels: none -> 52.9 us  [the longest x1 51 us: communicate(): pl.pallas_call(comm_kernel, name='exchange', out_shape=(jax.ShapeDtypeStr...]
  transfers between devices with their start and end apart: 2 -> 0, of which waited for: 2 -> 0; matrix products, arithmetic and copies ran while one was open for 0% -> 0% of each run, Pallas kernels for 0% -> 0%
where the time goes in v1:
time: 62.5 us; the launch traced here: 62.1 us
  Pallas kernels  52.9 us (85%)
  local copies, waits for them, and re-layouts  8.41 us (13%)
  between operations  0.72 us (1%)
    pallas_call x1, Pallas kernels, communicate(): pl.pallas_call(comm_kernel, name='exchange', out_shape=(jax.ShapeDtypeStr...  51 us
    unnamed x28, local copies, waits for them, and re-layouts  8.41 us
    pallas_call x1, Pallas kernels, local(): pl.pallas_call(update_kernel, name='update', out_shape=tuple((jax.ShapeDt...  1.88 us

profile of v1, /device:TPU:1, one launch (start us, length us, event | category | flops | bytes accessed | tf_op | source)
XLA Modules:
  0.0 62.1 jit_solution(4789154525430008458)
XLA Ops:
  0.6 0.0 copy-start
  0.6 1.0 %copy-done = f32[128,1024]{1,0:T(8,128)S(1)} copy-done((f32[128,1024]{1,0:T(8,128)S(1)}, f32[128,1024]{1,0:T(8,128)}, u32[]{:S(2)}) %copy-start) | copy-done | bytes 524312
  1.7 0.0 copy-start.2
  1.7 1.0 %copy-done.2 = f32[1,128,1024]{2,1,0:T(8,128)S(1)} copy-done((f32[1,128,1024]{2,1,0:T(8,128)S(1)}, f32[1,128,1024]{2,1,0:T(8,128)}, u32[]{:S(2)}) %copy-start.2) | copy-done | bytes 524312
  2.7 0.0 copy-start.4
  2.7 1.0 %copy-done.4 = f32[1,128,1024]{2,1,0:T(8,128)S(1)} copy-done((f32[1,128,1024]{2,1,0:T(8,128)S(1)}, f32[1,128,1024]{2,1,0:T(8,128)}, u32[]{:S(2)}) %copy-start.4) | copy-done | bytes 524312
  3.8 0.0 copy-start.6
  3.8 0.9 %copy-done.6 = f32[2,8,2048]{2,1,0:T(8,128)S(1)} copy-done((f32[2,8,2048]{2,1,0:T(8,128)S(1)}, f32[2,8,2048]{2,1,0:T(8,128)}, u32[]{:S(2)}) %copy-start.6) | copy-done | bytes 131096
  4.7 0.0 copy-start.8
  4.7 0.9 %copy-done.8 = f32[64,1024]{1,0:T(8,128)S(1)} copy-done((f32[64,1024]{1,0:T(8,128)S(1)}, f32[64,1024]{1,0:T(8,128)}, u32[]{:S(2)}) %copy-start.8) | copy-done | bytes 262168
  5.6 0.0 copy-start.9
  5.6 0.8 %copy-done.9 = f32[2,8,1024]{2,1,0:T(8,128)S(1)} copy-done((f32[2,8,1024]{2,1,0:T(8,128)S(1)}, f32[2,8,1024]{2,1,0:T(8,128)}, u32[]{:S(2)}) %copy-start.9) | copy-done | bytes 65560
  6.5 0.0 copy-start.10
  6.5 0.9 %copy-done.10 = f32[1,2,8,2048]{3,2,1,0:T(8,128)S(1)} copy-done((f32[1,2,8,2048]{3,2,1,0:T(8,128)S(1)}, f32[1,2,8,2048]{3,2,1,0:T(8,128)}, u32[]{:S(2)}) %copy-start.10) | copy-done | bytes 131096
  7.4 0.0 copy-start.12
  7.4 0.8 %copy-done.12 = f32[1,2,8,1024]{3,2,1,0:T(8,128)S(1)} copy-done((f32[1,2,8,1024]{3,2,1,0:T(8,128)S(1)}, f32[1,2,8,1024]{3,2,1,0:T(8,128)}, u32[]{:S(2)}) %copy-start.12) | copy-done | bytes 65560
  8.2 0.0 copy-start.1
  8.2 0.0 copy-start.3
  8.2 0.0 copy-start.5
  8.2 0.0 copy-start.7
  8.2 0.0 copy-start.11
  8.2 51.0 %exchange.1 = (f32[2,8,1024]{2,1,0:T(8,128)S(1)}, f32[2,8,2048]{2,1,0:T(8,128)S(1)}, f32[64,1024]{1,0:T(8,128)S(1)}, f32[128,64]{1,0:T(8,128)S(1)}) custom-call(f32[2,8,1024]{2,1,0:T(8,128)S(1)} %copy-done.9, f32[2,8,1024]{2,1,0:T(8,128)S(1)} %bitcast.10, f32[2,8,2048]{2,1,0:T(8,128)S(1)} %copy-done.6, f32[2,8,2048]{2,1,0:T(8,128)S(1)} %bitcast.9, ...), custom_call_target="tpu_custom_call" | custom-call | tf_op jit(solution)/shard_map/exchange/pallas_call | solution.py:251
  59.3 0.0 copy-done.1
  59.3 0.0 copy-done.3
  59.3 0.0 copy-done.5
  59.3 0.0 copy-done.7
  59.3 0.0 copy-done.11
  59.3 0.0 copy-start.13
  59.3 0.8 %copy-done.13 = f32[2,8,1024]{2,1,0:T(8,128)S(1)} copy-done((f32[2,8,1024]{2,1,0:T(8,128)S(1)}, f32[2,8,1024]{2,1,0:T(8,128)}, u32[]{:S(2)}) %copy-start.13) | copy-done | bytes 65560
  60.2 1.9 %update.1 = (f32[2,8,1024]{2,1,0:T(8,128)}, f32[2,8,1024]{2,1,0:T(8,128)}, f32[2,8,2048]{2,1,0:T(8,128)}, f32[2,8,2048]{2,1,0:T(8,128)}, f32[128,1024]{1,0:T(8,1...) custom-call(f32[2,8,1024]{2,1,0:T(8,128)S(1)} %get-tuple-element.18.sqs, f32[2,8,1024]{2,1,0:T(8,128)S(1)} %copy-done.9, ...), custom_call_target="tpu_custom_call" | custom-call | tf_op jit(solution)/shard_map/update/pallas_call | solution.py:308
Async XLA Ops:
  0.6 1.0 %copy-start = (f32[128,1024]{1,0:T(8,128)S(1)}, f32[128,1024]{1,0:T(8,128)}, u32[]{:S(2)}) copy-start(f32[128,1024]{1,0:T(8,128)} %ew.3) | copy-start | bytes 1572868
  1.7 1.0 %copy-start.2 = (f32[1,128,1024]{2,1,0:T(8,128)S(1)}, f32[1,128,1024]{2,1,0:T(8,128)}, u32[]{:S(2)}) copy-start(f32[1,128,1024]{2,1,0:T(8,128)} %param.18) | copy-start | bytes 1572868
  2.7 1.0 %copy-start.4 = (f32[1,128,1024]{2,1,0:T(8,128)S(1)}, f32[1,128,1024]{2,1,0:T(8,128)}, u32[]{:S(2)}) copy-start(f32[1,128,1024]{2,1,0:T(8,128)} %param.20) | copy-start | bytes 1572868
  3.8 0.9 %copy-start.6 = (f32[2,8,2048]{2,1,0:T(8,128)S(1)}, f32[2,8,2048]{2,1,0:T(8,128)}, u32[]{:S(2)}) copy-start(f32[2,8,2048]{2,1,0:T(8,128)} %brw.3) | copy-start | bytes 393220
  4.7 0.9 %copy-start.8 = (f32[64,1024]{1,0:T(8,128)S(1)}, f32[64,1024]{1,0:T(8,128)}, u32[]{:S(2)}) copy-start(f32[64,1024]{1,0:T(8,128)} %ws.1) | copy-start | bytes 786436
  5.6 0.8 %copy-start.9 = (f32[2,8,1024]{2,1,0:T(8,128)S(1)}, f32[2,8,1024]{2,1,0:T(8,128)}, u32[]{:S(2)}) copy-start(f32[2,8,1024]{2,1,0:T(8,128)} %sqw.3) | copy-start | bytes 196612
  6.5 0.9 %copy-start.10 = (f32[1,2,8,2048]{3,2,1,0:T(8,128)S(1)}, f32[1,2,8,2048]{3,2,1,0:T(8,128)}, u32[]{:S(2)}) copy-start(f32[1,2,8,2048]{3,2,1,0:T(8,128)} %param.15) | copy-start | bytes 393220
  7.4 0.8 %copy-start.12 = (f32[1,2,8,1024]{3,2,1,0:T(8,128)S(1)}, f32[1,2,8,1024]{3,2,1,0:T(8,128)}, u32[]{:S(2)}) copy-start(f32[1,2,8,1024]{3,2,1,0:T(8,128)} %param.12) | copy-start | bytes 196612
  8.2 51.1 %copy-start.1 = (f32[128,1024]{1,0:T(8,128)S(1)}, f32[128,1024]{1,0:T(8,128)}, u32[]{:S(2)}) copy-start(f32[128,1024]{1,0:T(8,128)} %ew.3) | copy-start | bytes 1572868
  8.2 51.1 %copy-start.3 = (f32[1,128,1024]{2,1,0:T(8,128)S(1)}, f32[1,128,1024]{2,1,0:T(8,128)}, u32[]{:S(2)}) copy-start(f32[1,128,1024]{2,1,0:T(8,128)} %param.18) | copy-start | bytes 1572868
  8.2 51.1 %copy-start.5 = (f32[1,128,1024]{2,1,0:T(8,128)S(1)}, f32[1,128,1024]{2,1,0:T(8,128)}, u32[]{:S(2)}) copy-start(f32[1,128,1024]{2,1,0:T(8,128)} %param.20) | copy-start | bytes 1572868
  8.2 51.1 %copy-start.7 = (f32[128,1024]{1,0:T(8,128)S(1)}, f32[128,1024]{1,0:T(8,128)}, u32[]{:S(2)}) copy-start(f32[128,1024]{1,0:T(8,128)} %em.1) | copy-start | bytes 1572868
  8.2 51.1 %copy-start.11 = (f32[2,8,2048]{2,1,0:T(8,128)S(1)}, f32[2,8,2048]{2,1,0:T(8,128)}, u32[]{:S(2)}) copy-start(f32[2,8,2048]{2,1,0:T(8,128)} %brm.1) | copy-start | bytes 393220
  59.3 0.8 %copy-start.13 = (f32[2,8,1024]{2,1,0:T(8,128)S(1)}, f32[2,8,1024]{2,1,0:T(8,128)}, u32[]{:S(2)}) copy-start(f32[2,8,1024]{2,1,0:T(8,128)} %sqm.1) | copy-start | bytes 196612

commit v2 on v1

--- a/solution.py
+++ b/solution.py
@@ -52,10 +52,10 @@
 
 
 def comm_kernel(
-    sqw, sqc, brw, brc, ew, ec, ee, ws,
-    sq_out, br_out, h_out, p_out,
-    vsqw, vsqc, vbrw, vbrc, vew, vec, vee, vws,
-    corr, corr_in, l_part, l_core, l_send, l_z, l_full, term, t_core, t_send, t_z, t_full,
+    sqw, sqc, brw, brc, ew, ec, ee, ws, sqm, brm, em,
+    o_squ, o_sqv, o_bru, o_brv, vew, vem, corr, p_out, h_out,
+    vsqw, vsqc, vbrw, vbrc, vsqm, vbrm, vec, vee, vws,
+    corr_in, l_part, l_in, l_full, term, t_core, t_send, t_z, t_full,
     h_part, h_in, h_zs, h_z, h_full, g_part, g_in, g_zs, g_z, g_full,
     load_sem, one_send, one_recv, rs_send, rs_recv, grs_send, grs_recv, z_send, z_recv, gz_send, gz_recv,
     ag_send, ag_recv, gag_send, gag_recv, fw_send, fw_recv,
@@ -66,29 +66,28 @@
     z, me = zhi * 8 + zlo, x * 4 + y
     other = 1 - core
 
+    def plane(dx, dy):
+        return lax.rem(x + dx, 4) * 4 + lax.rem(y + dy, 4)
+
+    def at_z(d):
+        return lax.rem(z + d, 16)
+
+    def dev(c, zz, q):
+        return (lax.div(zz, 8) * 2 + c, lax.rem(zz, 8) * 16 + q)
+
+    twin, far = dev(other, z, me), dev(core, at_z(8), me)
+    partners = [dev(other, at_z(8), me)] + [dev(core, at_z(d), me) for d in RING]
+    for dx, dy in PLANE:
+        partners += [dev(core, z, plane(dx, dy)), dev(other, z, plane(dx, dy))]
+    partners.append(twin)
+    barrier = pltpu.get_barrier_semaphore()
+    for device in partners:
+        pl.semaphore_signal(barrier, inc=1, device_id=device, device_id_type=MESH)
     loads = []
-    for i, (src, dst) in enumerate(((ew, vew), (ec, vec), (ee, vee), (ws, vws), (sqw, vsqw), (sqc, vsqc), (brw, vbrw), (brc, vbrc))):
+    for i, (src, dst) in enumerate(((ew, vew), (ec, vec), (ee, vee), (ws, vws), (sqw, vsqw), (sqc, vsqc), (brw, vbrw), (brc, vbrc), (sqm, vsqm), (brm, vbrm), (em, vem))):
         copy = pltpu.make_async_copy(src, dst, load_sem.at[i])
         copy.start()
         loads.append(copy)
-
-    def plane(dx, dy):
-        return lax.rem(x + dx, 4) * 4 + lax.rem(y + dy, 4)
-
-    def at_z(d):
-        return lax.rem(z + d, 16)
-
-    def dev(c, zz, q):
-        return (lax.div(zz, 8) * 2 + c, lax.rem(zz, 8) * 16 + q)
-
-    partners = [dev(other, z, me)]
-    for dx, dy in PLANE:
-        partners += [dev(core, z, plane(dx, dy)), dev(other, z, plane(dx, dy))]
-    for d in RING:
-        partners.append(dev(core, at_z(d), me))
-    barrier = pltpu.get_barrier_semaphore()
-    for device in partners:
-        pl.semaphore_signal(barrier, inc=1, device_id=device, device_id_type=MESH)
 
     sends = []
 
@@ -99,7 +98,7 @@
         return copy
 
     def arrived(dst, ss, rs):
-        pltpu.make_async_remote_copy(dst, dst, ss, rs, device_id=partners[0], device_id_type=MESH).wait_recv()
+        pltpu.make_async_remote_copy(dst, dst, ss, rs, device_id=twin, device_id_type=MESH).wait_recv()
 
     for i in range(4):
         loads[i].wait()
@@ -108,9 +107,12 @@
     l_part[0] = left[:32]
     l_part[1] = left[32:]
     pl.semaphore_wait(barrier, len(partners))
-    twin = partners[0]
-    send(l_part.at[other], l_core, one_send.at[0], one_recv.at[0], twin)
-    send(corr, corr_in, one_send.at[1], one_recv.at[1], twin)
+    peers = [(0, far), (1, dev(other, at_z(8), me)), (2, twin)]
+    for i, device in peers:
+        half = core if i == 0 else other
+        send(l_part.at[half], l_in.at[rep], one_send.at[i], one_recv.at[rep], device)
+    l_in[rep] = l_part[core]
+    send(corr, corr_in, one_send.at[3], one_recv.at[4], twin)
     for i in range(4, 8):
         loads[i].wait()
     for i in range(2):
@@ -118,22 +120,20 @@
         broad = vbrw[i] - vbrc[i]
         term[2 + 2 * i] = broad[:, :1024]
         term[3 + 2 * i] = broad[:, 1024:]
-    send(term.at[pl.ds(3 * other, 3)], t_core, one_send.at[2], one_recv.at[2], twin)
-    far = dev(core, at_z(8), me)
-    arrived(l_core, one_send.at[0], one_recv.at[0])
-    l_send[...] = l_part[core] + l_core[...]
-    send(l_send, l_z, one_send.at[3], one_recv.at[3], far)
-    arrived(t_core, one_send.at[2], one_recv.at[2])
+    send(term.at[pl.ds(3 * other, 3)], t_core, one_send.at[4], one_recv.at[5], twin)
+    arrived(t_core, one_send.at[4], one_recv.at[5])
     t_send[...] = term[pl.ds(3 * core, 3)] + t_core[...]
-    send(t_send, t_z, one_send.at[4], one_recv.at[4], far)
-    arrived(corr_in, one_send.at[1], one_recv.at[1])
-    total = vew
+    send(t_send, t_z, one_send.at[5], one_recv.at[6], far)
+    arrived(corr_in, one_send.at[3], one_recv.at[4])
+    total = vec
     total[...] = corr[...] + corr_in[...]
 
-    arrived(l_z, one_send.at[3], one_recv.at[3])
-    mine = (l_send[...] + l_z[...]) * 0.25
+    for k in range(1, 4):
+        r = lax.rem(rep + k, 4)
+        arrived(l_in.at[r], one_send.at[0], one_recv.at[r])
+    mine = ((l_in[0] + l_in[1]) + (l_in[2] + l_in[3])) * 0.25
     l_full[core] = mine
-    send(l_full.at[core], l_full.at[core], one_send.at[5], one_recv.at[5], twin)
+    send(l_full.at[core], l_full.at[core], one_send.at[6], one_recv.at[7], twin)
     for cb in range(4):
         block = dot(mine, total[:, 256 * cb : 256 * cb + 256]) * 0.25
         for rb in range(4):
@@ -143,7 +143,7 @@
         send(h_part.at[q], h_in.at[me], rs_send.at[i], rs_recv.at[me], dev(core, z, q))
     h_in[me] = h_part[me]
 
-    arrived(l_full.at[other], one_send.at[5], one_recv.at[5])
+    arrived(l_full.at[other], one_send.at[6], one_recv.at[7])
     left_all = jnp.concatenate([l_full[0], l_full[1]], axis=0)
     nothing = jnp.zeros_like(left_all)
     packed = dot_t(mine[:16], jnp.concatenate([left_all, nothing], axis=0)) + dot_t(mine[16:], jnp.concatenate([nothing, left_all], axis=0))
@@ -191,9 +191,9 @@
             send(mine_g, mine_g, gag_send.at[2 * i + k], gag_recv.at[slot], dev(c, z, q))
     send(mine_g, mine_g, gag_send.at[30], gag_recv.at[slot], twin)
 
-    arrived(t_z, one_send.at[4], one_recv.at[4])
+    arrived(t_z, one_send.at[5], one_recv.at[6])
     t_full[pl.ds(3 * core, 3)] = (t_send[...] + t_z[...]) * 0.25
-    send(t_full.at[pl.ds(3 * core, 3)], t_full.at[pl.ds(3 * core, 3)], one_send.at[6], one_recv.at[6], twin)
+    send(t_full.at[pl.ds(3 * core, 3)], t_full.at[pl.ds(3 * core, 3)], one_send.at[7], one_recv.at[8], twin)
 
     for d in RING:
         peer = at_z(d)
@@ -227,50 +227,46 @@
         q = plane(dx, dy)
         arrived(h_full.at[core, q], ag_send.at[i], ag_recv.at[q])
         send(h_full.at[core, q], h_full.at[core, q], fw_send.at[i], fw_recv.at[q], twin)
-    arrived(t_full.at[pl.ds(3 * other, 3)], one_send.at[6], one_recv.at[6])
+    arrived(t_full.at[pl.ds(3 * other, 3)], one_send.at[7], one_recv.at[8])
+    for i in range(8, 11):
+        loads[i].wait()
     for i in range(2):
-        sq_out[i] = t_full[i]
-        br_out[i, :, :1024] = t_full[2 + 2 * i]
-        br_out[i, :, 1024:] = t_full[3 + 2 * i]
+        o_squ[i], o_sqv[i] = nesterov(vsqw[i], t_full[i], vsqm[i])
+        for k in range(2):
+            half = slice(1024 * k, 1024 * k + 1024)
+            o_bru[i, :, half], o_brv[i, :, half] = nesterov(vbrw[i, :, half], t_full[2 + 2 * i + k], vbrm[i, :, half])
     for i, (dx, dy) in enumerate(PLANE):
         q = plane(dx, dy)
         arrived(h_full.at[other, q], fw_send.at[i], fw_recv.at[q])
     arrived(h_full.at[other, me], fw_send.at[15], fw_recv.at[me])
-    for c in range(2):
-        for rb in range(4):
-            for cb in range(4):
-                h_out[32 * c + 8 * rb : 32 * c + 8 * rb + 8, 256 * cb : 256 * cb + 256] = h_full[c, 4 * rb + cb]
+    h_out[...] = h_full[...]
     for copy in sends:
         copy.wait_send()
 
 
-def communicate(sqw, sqc, brw, brc, ew, ec, ee, ws):
+def communicate(*args):
     f32 = jnp.float32
     vmem = lambda *shape: pltpu.VMEM(shape, f32)
     dma = lambda n: pltpu.SemaphoreType.DMA((n,))
+    shapes = [(2, 8, 1024)] * 2 + [(2, 8, 2048)] * 2 + [(128, 1024)] * 3 + [(128, 64), (2, 16, 8, 256)]
     return pl.pallas_call(
         comm_kernel,
         name="exchange",
-        out_shape=(
-            jax.ShapeDtypeStruct((2, 8, 1024), f32),
-            jax.ShapeDtypeStruct((2, 8, 2048), f32),
-            jax.ShapeDtypeStruct((64, 1024), f32),
-            jax.ShapeDtypeStruct((128, 64), f32),
-        ),
-        in_specs=[pl.BlockSpec(memory_space=pl.ANY)] * 8,
-        out_specs=tuple(pl.BlockSpec(memory_space=pltpu.VMEM) for _ in range(4)),
+        out_shape=tuple(jax.ShapeDtypeStruct(s, f32) for s in shapes),
+        in_specs=[pl.BlockSpec(memory_space=pltpu.HBM)] * 11,
+        out_specs=tuple(pl.BlockSpec(memory_space=pltpu.VMEM) for _ in shapes),
         scratch_shapes=[
-            vmem(2, 8, 1024), vmem(2, 8, 1024), vmem(2, 8, 2048), vmem(2, 8, 2048),
-            vmem(128, 1024), vmem(128, 1024), vmem(128, 1024), vmem(64, 1024),
-            vmem(128, 1024), vmem(128, 1024), vmem(2, 32, 128), vmem(32, 128), vmem(32, 128), vmem(32, 128), vmem(2, 32, 128),
+            vmem(2, 8, 1024), vmem(2, 8, 1024), vmem(2, 8, 2048), vmem(2, 8, 2048), vmem(2, 8, 1024), vmem(2, 8, 2048),
+            vmem(128, 1024), vmem(128, 1024), vmem(64, 1024),
+            vmem(128, 1024), vmem(2, 32, 128), vmem(4, 32, 128), vmem(2, 32, 128),
             vmem(6, 8, 1024), vmem(3, 8, 1024), vmem(3, 8, 1024), vmem(3, 8, 1024), vmem(6, 8, 1024),
             vmem(16, 8, 256), vmem(16, 8, 256), vmem(8, 256), vmem(16, 8, 256), vmem(2, 16, 8, 256),
             vmem(16, 1, 128), vmem(16, 1, 128), vmem(1, 128), vmem(8, 1, 128), vmem(2, 16, 1, 128),
-            dma(8), dma(7), dma(7), dma(15), dma(16), dma(15), dma(16), dma(16), dma(16), dma(8), dma(8),
+            dma(11), dma(8), dma(11), dma(15), dma(16), dma(15), dma(16), dma(16), dma(16), dma(8), dma(8),
             dma(15), dma(16), dma(31), dma(32), dma(16), dma(16),
         ],
         compiler_params=pltpu.CompilerParams(collective_id=0, has_side_effects=True, vmem_limit_bytes=16 << 20),
-    )(sqw, sqc, brw, brc, ew, ec, ee, ws)
+    )(*(pltpu.with_memory_space_constraint(v, pltpu.HBM) for v in args))
 
 
 def nesterov(weights, gradient, moment):
@@ -278,14 +274,21 @@
     return (weights - outer_rate * (gradient + momentum_decay * velocity), velocity)
 
 
-def update_kernel(sqs, sqw, sqm, brs, brw, brm, ew, ec, em, ee, p, h, squ, sqv, bru, brv, eu, ev, er):
-    squ[...], sqv[...] = nesterov(sqw[...], sqs[...], sqm[...])
-    bru[...], brv[...] = nesterov(brw[...], brs[...], brm[...])
+def update_kernel(squ, sqv, bru, brv, ew, em, corr, p, h, o_squ, o_sqv, o_bru, o_brv, o_eu, o_ev, o_er, eu, ev, er, sems):
+    copies = [pltpu.make_async_copy(src, dst, sems.at[i]) for i, (src, dst) in enumerate(((squ, o_squ), (sqv, o_sqv), (bru, o_bru), (brv, o_brv)))]
+    for copy in copies:
+        copy.start()
     for cb in range(4):
         at = (slice(None), slice(256 * cb, 256 * cb + 256))
-        step = dot(p[...], h[at])
+        step = dot(p[...], jnp.concatenate([h[c, 4 * rb + cb] for c in range(2) for rb in range(4)], axis=0))
         eu[at], ev[at] = nesterov(ew[at], step, em[at])
-        er[at] = ew[at] - ec[at] + ee[at] - step
+        er[at] = corr[at] - step
+        for i, (src, dst) in enumerate(((eu, o_eu), (ev, o_ev), (er, o_er))):
+            copy = pltpu.make_async_copy(src.at[at], dst.at[at], sems.at[4 + 3 * cb + i])
+            copy.start()
+            copies.append(copy)
+    for copy in copies:
+        copy.wait()
 
 
 def local(
@@ -301,19 +304,20 @@
     embed_error,
     warm_start,
 ):
-    sq_sum, br_sum, h, p = communicate(
-        square_weights, square_copies[0], broad_weights, broad_copies[0], embed_weights, embed_copies[0], embed_error[0], warm_start
+    ready = communicate(
+        square_weights, square_copies[0], broad_weights, broad_copies[0], embed_weights, embed_copies[0], embed_error[0], warm_start,
+        square_moment, broad_moment, embed_moment,
     )
     shapes = [square_weights.shape] * 2 + [broad_weights.shape] * 2 + [embed_weights.shape] * 3
     outs = pl.pallas_call(
         update_kernel,
         name="update",
         out_shape=tuple(jax.ShapeDtypeStruct(s, jnp.float32) for s in shapes),
+        in_specs=[pl.BlockSpec(memory_space=pltpu.VMEM)] * 9,
+        out_specs=tuple(pl.BlockSpec(memory_space=pltpu.HBM) for _ in shapes),
+        scratch_shapes=[pltpu.VMEM((128, 1024), jnp.float32)] * 3 + [pltpu.SemaphoreType.DMA((16,))],
         compiler_params=pltpu.CompilerParams(vmem_limit_bytes=16 << 20),
-    )(
-        sq_sum, square_weights, square_moment, br_sum, broad_weights, broad_moment,
-        embed_weights, embed_copies[0], embed_moment, embed_error[0], p, h,
-    )
+    )(*ready)
     return (*outs[:6], outs[6][None])
 
 

time: 62.5 us -> 52.4 us (0.84)
  local copies, waits for them, and re-layouts: 8.41 us -> 0 us
  Pallas kernels: 52.9 us -> 51.6 us
    unnamed x28 -> x0, local copies, waits for them, and re-layouts: 8.41 us -> none
    pallas_call x1, Pallas kernels: 51 us -> 50 us  [communicate(): pl.pallas_call(comm_kernel, name='exchange', out_shape=tuple((jax.ShapeDt...]
where the time goes in v2:
time: 52.4 us; the launch traced here: 52.3 us
  Pallas kernels  51.6 us (98%)
  between operations  0.64 us (1%)
    pallas_call x1, Pallas kernels, communicate(): pl.pallas_call(comm_kernel, name='exchange', out_shape=tuple((jax.ShapeDt...  50 us
    pallas_call x1, Pallas kernels, local(): pl.pallas_call(update_kernel, name='update', out_shape=tuple((jax.ShapeDt...  1.67 us

profile of v2, /device:TPU:1, one launch (start us, length us, event | category | flops | bytes accessed | tf_op | source)
XLA Modules:
  0.0 52.3 jit_solution(8624268381044084173)
XLA Ops:
  0.6 50.0 %exchange.1 = (f32[2,8,1024]{2,1,0:T(8,128)S(1)}, f32[2,8,1024]{2,1,0:T(8,128)S(1)}, f32[2,8,2048]{2,1,0:T(8,128)S(1)}, f32[2,8,2048]{2,1,0:T(8,128)S(1)}, f32[1...) custom-call(f32[2,8,1024]{2,1,0:T(8,128)} %sqw.1, ...), custom_call_target="tpu_custom_call" | custom-call | tf_op jit(solution)/shard_map/exchange/pallas_call | solution.py:252
  50.6 1.7 %update.1 = (f32[2,8,1024]{2,1,0:T(8,128)}, f32[2,8,1024]{2,1,0:T(8,128)}, f32[2,8,2048]{2,1,0:T(8,128)}, f32[2,8,2048]{2,1,0:T(8,128)}, f32[128,1024]{1,0:T(8,1...) custom-call(f32[2,8,1024]{2,1,0:T(8,128)S(1)} %get-tuple-element.23.squ, f32[2,8,1024]{2,1,0:T(8,128)S(1)} %get-tuple-element.24.sqv, ...), custom_call_target="tpu_custom_call" | custom-call | tf_op jit(solution)/shard_map/update/pallas_call | solution.py:312

commit v3 on v2

v3 whole, which is shorter than its diff:
```python
import jax
import jax.numpy as jnp
from jax import lax
from jax.experimental import pallas as pl
from jax.experimental.pallas import tpu as pltpu
from jax.sharding import PartitionSpec as P

outer_rate = 0.7
momentum_decay = 0.9
MESH = pl.DeviceIdType.MESH
HIGHEST = lax.Precision.HIGHEST


def hops(dx, dy):
    return min(dx, 4 - dx) + min(dy, 4 - dy)


PLANE = sorted(((dx, dy) for dx in range(4) for dy in range(4) if dx or dy), key=lambda d: -hops(*d))
FAR = sum(hops(*d) > 0 for d in PLANE)
RING = sorted(range(1, 16), key=lambda d: -min(d, 16 - d))


def dot(a, b):
    return jnp.dot(a, b, precision=HIGHEST, preferred_element_type=jnp.float32)


def dot_t(a, b):
    return lax.dot_general(a, b, (((1,), (1,)), ((), ())), precision=HIGHEST, preferred_element_type=jnp.float32)


def sub(v, j):
    return jnp.broadcast_to(v[j : j + 1, :], v.shape)


def lower_inverse(a):
    rows = lax.broadcasted_iota(jnp.int32, (8, 128), 0)
    scale = []
    for kb in range(8):
        cols = {}
        for j in range(8):
            lane = 64 + 8 * kb + j
            for b in range(kb, 8):
                cols[b, j] = jnp.broadcast_to(a[b][:, lane : lane + 1], (8, 128))
        inv_pivots = jnp.ones((8, 128), jnp.float32)
        for j in range(8):
            inv = 1.0 / sub(cols[kb, j], j)
            inv_pivots = jnp.where(rows == j, inv, inv_pivots)
            row = sub(a[kb], j)
            later = [sub(cols[kb, i], j) for i in range(j + 1, 8)]
            for b in range(kb, 8):
                factor = cols[b, j] * inv
                if b == kb:
                    factor = jnp.where(rows > j, factor, 0.0)
                a[b] = a[b] - factor * row
                for i in range(j + 1, 8):
                    cols[b, i] = cols[b, i] - factor * later[i - j - 1]
        scale.append(jnp.sqrt(inv_pivots))
    return [a[b] * scale[b] for b in range(8)]


def comm_kernel(
    sqw, sqc, brw, brc, ew, ec, ee, ws, sqm, brm, em,
    o_squ, o_sqv, o_bru, o_brv, vew, vem, corr, p_out, h_out,
    vsqw, vsqc, vbrw, vbrc, vsqm, vbrm, vec, vee, vws,
    corr_in, l_part, l_twin, l_chip, l_in, l_relay, l_full, g_side, term, t_core, t_send, t_relay, t_z, t_full,
    h_part, h_in, h_zs, h_z, h_full, g_part, g_in, g_zs, g_z, g_full,
    load_sem, sent, got, piece_sem,
):
    rep, inn = lax.axis_index("replica"), lax.axis_index("inner")
    core, zhi = lax.rem(rep, 2), lax.div(rep, 2)
    zlo, x, y = lax.div(inn, 16), lax.rem(lax.div(inn, 4), 4), lax.rem(inn, 4)
    z, me = zhi * 8 + zlo, x * 4 + y
    other = 1 - core

    def plane(dx, dy):
        return lax.rem(x + dx, 4) * 4 + lax.rem(y + dy, 4)

    def at_z(d):
        return lax.rem(z + d, 16)

    def dev(c, zz, q):
        return (lax.div(zz, 8) * 2 + c, lax.rem(zz, 8) * 16 + q)

    twin, ahead, behind = dev(other, z, me), at_z(4), at_z(12)
    partners = [dev(other, ahead, me), dev(other, behind, me)] + [dev(core, at_z(d), me) for d in (4, 12, 3, 13, 2, 14, 1, 15)]
    for dx, dy in PLANE:
        partners += [dev(core, z, plane(dx, dy)), dev(other, z, plane(dx, dy))]
    partners.append(twin)
    barrier = pltpu.get_barrier_semaphore()
    for device in partners:
        pl.semaphore_signal(barrier, inc=1, device_id=device, device_id_type=MESH)
    loads = []
    for i, (src, dst) in enumerate(((ew, vew), (ec, vec), (ee, vee), (ws, vws), (sqw, vsqw), (sqc, vsqc), (brw, vbrw), (brc, vbrc), (sqm, vsqm), (brm, vbrm), (em, vem))):
        copy = pltpu.make_async_copy(src, dst, load_sem.at[i])
        copy.start()
        loads.append(copy)

    def send(src, dst, stage, device, arrival=None):
        pltpu.make_async_remote_copy(src, dst, sent.at[stage], got.at[stage] if arrival is None else arrival, device_id=device, device_id_type=MESH).start()

    def copies(ref, stage, arrival=None):
        return pltpu.make_async_remote_copy(ref, ref, sent.at[stage], got.at[stage] if arrival is None else arrival, device_id=twin, device_id_type=MESH)

    def arrived(ref, stage):
        copies(ref, stage).wait_recv()

    def left(ref, stage):
        copies(ref, stage).wait_send()

    def first(ref, n):
        return ref.at[pl.ds(0, n)]

    def added(ref, n):
        out = ref[0]
        for i in range(1, n):
            out = out + ref[i]
        return out

    for i in range(4):
        loads[i].wait()
    corr[...] = vew[...] - vec[...] + vee[...]
    part = dot_t(vws[...], corr[...])
    l_part[0] = part[:32]
    l_part[1] = part[32:]
    pl.semaphore_wait(barrier, len(partners))
    send(l_part.at[0], l_relay.at[0], 13, dev(core, ahead, me))
    send(l_part.at[1], l_relay.at[1], 14, dev(core, behind, me))
    send(l_part, l_twin, 17, twin)
    for i in range(4, 8):
        loads[i].wait()
    for i in range(2):
        for k in range(2):
            half = slice(512 * k, 512 * k + 512)
            term[2 * i + k] = vsqw[i, :, half] - vsqc[i, :, half]
        for k in range(4):
            half = slice(512 * k, 512 * k + 512)
            term[4 + 4 * i + k] = vbrw[i, :, half] - vbrc[i, :, half]
    mine_t, other_t = pl.ds(6 * core, 6), pl.ds(6 * other, 6)
    send(term.at[other_t], t_core, 1, twin)
    send(corr, corr_in, 2, twin)
    arrived(t_core, 1)
    t_send[...] = term[mine_t] + t_core[...]
    low, high = pl.ds(0, 3), pl.ds(3, 3)
    send(t_send.at[low], t_relay.at[0], 15, dev(core, ahead, me))
    send(t_send.at[high], t_relay.at[1], 16, dev(core, behind, me))
    arrived(l_relay.at[0], 13)
    send(l_relay.at[0], l_in.at[core], 0, dev(0, ahead, me))
    arrived(l_relay.at[1], 14)
    send(l_relay.at[1], l_in.at[core], 0, dev(1, behind, me))
    arrived(corr_in, 2)
    total = vec
    total[...] = corr[...] + corr_in[...]
    left(t_core, 1)
    left(corr, 2)
    arrived(l_twin, 17)
    left(l_part, 17)
    l_chip[...] = l_part[...] + l_twin[...]
    chip = jnp.concatenate([l_chip[0], l_chip[1]], axis=0) * 0.25
    nothing = jnp.zeros_like(chip)
    g_side[0] = jnp.concatenate([chip, nothing], axis=0)
    g_side[1] = jnp.concatenate([nothing, chip], axis=0)
    left(l_part.at[0], 13)
    left(l_part.at[1], 14)
    arrived(t_relay.at[0], 15)
    send(t_relay.at[0], t_z.at[low], 3, dev(core, ahead, me))
    arrived(t_relay.at[1], 16)
    send(t_relay.at[1], t_z.at[high], 3, dev(core, behind, me))
    left(t_send.at[low], 15)
    left(t_send.at[high], 16)

    arrived(l_in, 0)
    mine = (l_chip[core] + (l_in[0] + l_in[1])) * 0.25
    for cb in range(4):
        block = dot(mine, total[:, 256 * cb : 256 * cb + 256]) * 0.25
        for rb in range(4):
            h_part[4 * rb + cb] = block[8 * rb : 8 * rb + 8]
    for dx, dy in PLANE:
        q = plane(dx, dy)
        send(h_part.at[q], h_in.at[me], 5, dev(core, z, q))
    h_in[me] = h_part[me]

    packed = dot_t(mine[:16], g_side[0]) + dot_t(mine[16:], g_side[1])
    for i in range(16):
        g_part[i] = packed[i : i + 1]
    for dx, dy in PLANE:
        q = plane(dx, dy)
        send(g_part.at[q], g_in.at[me], 6, dev(core, z, q))
    g_in[me] = g_part[me]
    l_full[core] = mine
    send(l_full.at[core], l_full.at[core], 4, twin)
    left(l_in, 0)

    arrived(first(g_in, 15), 6)
    g_sum = added(g_in, 16)
    g_zs[...] = g_sum
    g_z[z] = g_sum
    for d in RING:
        send(g_zs, g_z.at[z], 8, dev(core, at_z(d), me))
    arrived(first(h_in, 15), 5)
    h_sum = added(h_in, 16)
    h_zs[...] = h_sum
    h_z[z] = h_sum
    for d in RING:
        send(h_zs, h_z.at[z], 7, dev(core, at_z(d), me))
    left(first(h_in, 15), 5)
    left(first(g_in, 15), 6)

    arrived(t_z, 3)
    t_full[mine_t] = (t_send[...] + t_z[...]) * 0.25
    send(t_full.at[mine_t], t_full.at[mine_t], 9, twin)
    left(t_send, 3)
    for i in range(8, 11):
        loads[i].wait()

    arrived(l_full.at[other], 4)
    left(l_full.at[core], 4)
    arrived(first(g_z, 15), 8)
    slot = core * 16 + me
    g_full[slot] = added(g_z, 16)
    for dx, dy in PLANE:
        for c in (core, other):
            send(g_full.at[slot], g_full.at[slot], 10, dev(c, z, plane(dx, dy)))
    send(g_full.at[slot], g_full.at[slot], 10, twin)
    left(first(g_z, 15), 8)

    arrived(first(h_z, 15), 7)
    h_full[slot] = added(h_z, 16)
    for dx, dy in PLANE:
        send(h_full.at[slot], h_full.at[slot], 11, dev(core, z, plane(dx, dy)), piece_sem.at[me])
        if hops(dx, dy) > 0:
            send(h_full.at[slot], h_full.at[slot], 11, dev(other, z, plane(dx, dy)), got.at[12])
    send(h_full.at[slot], h_full.at[slot], 12, twin)
    left(first(h_z, 15), 7)

    arrived(t_full.at[other_t], 9)
    left(t_full.at[mine_t], 9)
    for i in range(2):
        for k in range(2):
            half = slice(512 * k, 512 * k + 512)
            o_squ[i, :, half], o_sqv[i, :, half] = nesterov(vsqw[i, :, half], t_full[2 * i + k], vsqm[i, :, half])
        for k in range(4):
            half = slice(512 * k, 512 * k + 512)
            o_bru[i, :, half], o_brv[i, :, half] = nesterov(vbrw[i, :, half], t_full[4 + 4 * i + k], vbrm[i, :, half])

    arrived(first(g_full, 31), 10)
    lanes = lax.broadcasted_iota(jnp.int32, (8, 128), 1)
    rows = lax.broadcasted_iota(jnp.int32, (8, 128), 0)
    blocks = [None] * 8
    for c in range(2):
        for half in range(2):
            tile = jnp.concatenate([g_full[16 * c + 8 * half + i] for i in range(8)], axis=0)
            blocks[4 * c + half] = pltpu.roll(tile, 64, 1)
            blocks[4 * c + 2 + half] = tile
    for b in range(8):
        blocks[b] = jnp.where(lanes >= 64, blocks[b], jnp.where(lanes == rows + 8 * b, 1.0, 0.0))
    inverse = jnp.concatenate(lower_inverse(blocks), axis=0)[:, :64]
    p_out[...] = dot(dot_t(jnp.concatenate([l_full[0], l_full[1]], axis=0).T, inverse), inverse)
    left(first(g_full, 31), 10)

    for dx, dy in reversed(PLANE):
        q = plane(dx, dy)
        at = core * 16 + q
        copies(h_full.at[at], 11, piece_sem.at[q]).wait_recv()
        if hops(dx, dy) <= 0:
            send(h_full.at[at], h_full.at[at], 12, twin)
    left(first(h_full, 15 + FAR), 11)
    arrived(first(h_full, 16), 12)
    h_out[...] = h_full[...]
    left(first(h_full, 16 - FAR), 12)


def communicate(*args):
    f32 = jnp.float32
    vmem = lambda *shape: pltpu.VMEM(shape, f32)
    dma = lambda n: pltpu.SemaphoreType.DMA((n,))
    shapes = [(2, 8, 1024)] * 2 + [(2, 8, 2048)] * 2 + [(128, 1024)] * 3 + [(128, 64), (32, 8, 256)]
    return pl.pallas_call(
        comm_kernel,
        name="exchange",
        out_shape=tuple(jax.ShapeDtypeStruct(s, f32) for s in shapes),
        in_specs=[pl.BlockSpec(memory_space=pltpu.HBM)] * 11,
        out_specs=tuple(pl.BlockSpec(memory_space=pltpu.VMEM) for _ in shapes),
        scratch_shapes=[
            vmem(2, 8, 1024), vmem(2, 8, 1024), vmem(2, 8, 2048), vmem(2, 8, 2048), vmem(2, 8, 1024), vmem(2, 8, 2048),
            vmem(128, 1024), vmem(128, 1024), vmem(64, 1024),
            vmem(128, 1024), vmem(2, 32, 128), vmem(2, 32, 128), vmem(2, 32, 128), vmem(2, 32, 128), vmem(2, 32, 128), vmem(2, 32, 128), vmem(2, 128, 128),
            vmem(12, 8, 512), vmem(6, 8, 512), vmem(6, 8, 512), vmem(2, 3, 8, 512), vmem(6, 8, 512), vmem(12, 8, 512),
            vmem(16, 8, 256), vmem(16, 8, 256), vmem(8, 256), vmem(16, 8, 256), vmem(32, 8, 256),
            vmem(16, 1, 128), vmem(16, 1, 128), vmem(1, 128), vmem(16, 1, 128), vmem(32, 1, 128),
            dma(11), dma(18), dma(18), dma(16),
        ],
        compiler_params=pltpu.CompilerParams(collective_id=0, has_side_effects=True, vmem_limit_bytes=16 << 20),
    )(*(pltpu.with_memory_space_constraint(v, pltpu.HBM) for v in args))


def nesterov(weights, gradient, moment):
    velocity = momentum_decay * moment + gradient
    return (weights - outer_rate * (gradient + momentum_decay * velocity), velocity)


def update_kernel(squ, sqv, bru, brv, ew, em, corr, p, h, o_squ, o_sqv, o_bru, o_brv, o_eu, o_ev, o_er, eu, ev, er, sems):
    copies = [pltpu.make_async_copy(src, dst, sems.at[i]) for i, (src, dst) in enumerate(((squ, o_squ), (sqv, o_sqv), (bru, o_bru), (brv, o_brv)))]
    for copy in copies:
        copy.start()
    for cb in range(4):
        at = (slice(None), slice(256 * cb, 256 * cb + 256))
        step = dot(p[...], jnp.concatenate([h[16 * c + 4 * rb + cb] for c in range(2) for rb in range(4)], axis=0))
        eu[at], ev[at] = nesterov(ew[at], step, em[at])
        er[at] = corr[at] - step
        for i, (src, dst) in enumerate(((eu, o_eu), (ev, o_ev), (er, o_er))):
            copy = pltpu.make_async_copy(src.at[at], dst.at[at], sems.at[4 + 3 * cb + i])
            copy.start()
            copies.append(copy)
    for copy in copies:
        copy.wait()


def local(
    square_weights,
    square_copies,
    square_moment,
    broad_weights,
    broad_copies,
    broad_moment,
    embed_weights,
    embed_copies,
    embed_moment,
    embed_error,
    warm_start,
):
    ready = communicate(
        square_weights, square_copies[0], broad_weights, broad_copies[0], embed_weights, embed_copies[0], embed_error[0], warm_start,
        square_moment, broad_moment, embed_moment,
    )
    shapes = [square_weights.shape] * 2 + [broad_weights.shape] * 2 + [embed_weights.shape] * 3
    outs = pl.pallas_call(
        update_kernel,
        name="update",
        out_shape=tuple(jax.ShapeDtypeStruct(s, jnp.float32) for s in shapes),
        in_specs=[pl.BlockSpec(memory_space=pltpu.VMEM)] * 9,
        out_specs=tuple(pl.BlockSpec(memory_space=pltpu.HBM) for _ in shapes),
        scratch_shapes=[pltpu.VMEM((128, 1024), jnp.float32)] * 3 + [pltpu.SemaphoreType.DMA((16,))],
        compiler_params=pltpu.CompilerParams(vmem_limit_bytes=16 << 20),
    )(*ready)
    return (*outs[:6], outs[6][None])


def solution(mesh):
    in_specs = (
        P(None, "inner", None),
        P("replica", None, "inner", None),
        P(None, "inner", None),
        P(None, "inner", None),
        P("replica", None, "inner", None),
        P(None, "inner", None),
        P("inner", None),
        P("replica", "inner", None),
        P("inner", None),
        P("replica", "inner", None),
        P(),
    )
    out_specs = (
        P(None, "inner", None),
        P(None, "inner", None),
        P(None, "inner", None),
        P(None, "inner", None),
        P("inner", None),
        P("inner", None),
        P("replica", "inner", None),
    )
    return jax.shard_map(local, mesh=mesh, in_specs=in_specs, out_specs=out_specs, check_vma=False)
```

time: 52.4 us -> 49.8 us (0.950)
  Pallas kernels: 51.6 us -> 49 us
    pallas_call x1, Pallas kernels: 50 us -> 47.3 us  [communicate(): pl.pallas_call(comm_kernel, name='exchange', out_shape=tuple((jax.ShapeDt...]
where the time goes in v3:
time: 49.8 us; the launch traced here: 49.6 us
  Pallas kernels  49 us (98%)
  between operations  0.64 us (1%)
    pallas_call x1, Pallas kernels, communicate(): pl.pallas_call(comm_kernel, name='exchange', out_shape=tuple((jax.ShapeDt...  47.3 us
    pallas_call x1, Pallas kernels, local(): pl.pallas_call(update_kernel, name='update', out_shape=tuple((jax.ShapeDt...  1.67 us

profile of v3, /device:TPU:1, one launch (start us, length us, event | category | flops | bytes accessed | tf_op | source)
XLA Modules:
  0.0 49.6 jit_solution(2959455571249661754)
XLA Ops:
  0.6 47.3 %exchange.1 = (f32[2,8,1024]{2,1,0:T(8,128)S(1)}, f32[2,8,1024]{2,1,0:T(8,128)S(1)}, f32[2,8,2048]{2,1,0:T(8,128)S(1)}, f32[2,8,2048]{2,1,0:T(8,128)S(1)}, f32[1...) custom-call(f32[2,8,1024]{2,1,0:T(8,128)} %sqw.1, ...), custom_call_target="tpu_custom_call" | custom-call | tf_op jit(solution)/shard_map/exchange/pallas_call | solution.py:277
  48.0 1.7 %update.1 = (f32[2,8,1024]{2,1,0:T(8,128)}, f32[2,8,1024]{2,1,0:T(8,128)}, f32[2,8,2048]{2,1,0:T(8,128)}, f32[2,8,2048]{2,1,0:T(8,128)}, f32[128,1024]{1,0:T(8,1...) custom-call(f32[2,8,1024]{2,1,0:T(8,128)S(1)} %get-tuple-element.23.squ, f32[2,8,1024]{2,1,0:T(8,128)S(1)} %get-tuple-element.24.sqv, ...), custom_call_target="tpu_custom_call" | custom-call | tf_op jit(solution)/shard_map/update/pallas_call | solution.py:336

commit v4 on v3

--- a/solution.py
+++ b/solution.py
@@ -16,7 +16,6 @@
 
 
 PLANE = sorted(((dx, dy) for dx in range(4) for dy in range(4) if dx or dy), key=lambda d: -hops(*d))
-FAR = sum(hops(*d) > 0 for d in PLANE)
 RING = sorted(range(1, 16), key=lambda d: -min(d, 16 - d))
 
 
@@ -64,7 +63,7 @@
     vsqw, vsqc, vbrw, vbrc, vsqm, vbrm, vec, vee, vws,
     corr_in, l_part, l_twin, l_chip, l_in, l_relay, l_full, g_side, term, t_core, t_send, t_relay, t_z, t_full,
     h_part, h_in, h_zs, h_z, h_full, g_part, g_in, g_zs, g_z, g_full,
-    load_sem, sent, got, piece_sem,
+    load_sem, sent, got,
 ):
     rep, inn = lax.axis_index("replica"), lax.axis_index("inner")
     core, zhi = lax.rem(rep, 2), lax.div(rep, 2)
@@ -86,14 +85,19 @@
     for dx, dy in PLANE:
         partners += [dev(core, z, plane(dx, dy)), dev(other, z, plane(dx, dy))]
     partners.append(twin)
+    loads = [
+        pltpu.make_async_copy(src, dst, load_sem.at[i])
+        for i, (src, dst) in enumerate((
+            (ew, vew), (ec, vec), (ee, vee), (ws, vws), (sqw, vsqw), (sqc, vsqc), (brw, vbrw), (brc, vbrc), (sqm, vsqm), (brm, vbrm), (em, vem)
+        ))
+    ]
+    for i in range(4):
+        loads[i].start()
     barrier = pltpu.get_barrier_semaphore()
     for device in partners:
         pl.semaphore_signal(barrier, inc=1, device_id=device, device_id_type=MESH)
-    loads = []
-    for i, (src, dst) in enumerate(((ew, vew), (ec, vec), (ee, vee), (ws, vws), (sqw, vsqw), (sqc, vsqc), (brw, vbrw), (brc, vbrc), (sqm, vsqm), (brm, vbrm), (em, vem))):
-        copy = pltpu.make_async_copy(src, dst, load_sem.at[i])
-        copy.start()
-        loads.append(copy)
+    for i in range(4, 11):
+        loads[i].start()
 
     def send(src, dst, stage, device, arrival=None):
         pltpu.make_async_remote_copy(src, dst, sent.at[stage], got.at[stage] if arrival is None else arrival, device_id=device, device_id_type=MESH).start()
@@ -123,6 +127,7 @@
     l_part[0] = part[:32]
     l_part[1] = part[32:]
     pl.semaphore_wait(barrier, len(partners))
+
     send(l_part.at[0], l_relay.at[0], 13, dev(core, ahead, me))
     send(l_part.at[1], l_relay.at[1], 14, dev(core, behind, me))
     send(l_part, l_twin, 17, twin)
@@ -159,36 +164,35 @@
     nothing = jnp.zeros_like(chip)
     g_side[0] = jnp.concatenate([chip, nothing], axis=0)
     g_side[1] = jnp.concatenate([nothing, chip], axis=0)
+
     left(l_part.at[0], 13)
     left(l_part.at[1], 14)
+    arrived(l_in, 0)
+    mine = (l_chip[core] + (l_in[0] + l_in[1])) * 0.25
+    packed = dot_t(mine[:16], g_side[0]) + dot_t(mine[16:], g_side[1])
+    for i in range(16):
+        g_part[i] = packed[i : i + 1]
+    for dx, dy in PLANE:
+        q = plane(dx, dy)
+        send(g_part.at[q], g_in.at[me], 6, dev(core, z, q))
+    for cb in range(4):
+        block = dot(mine, total[:, 256 * cb : 256 * cb + 256]) * 0.25
+        for rb in range(4):
+            h_part[4 * rb + cb] = block[8 * rb : 8 * rb + 8]
+    for dx, dy in PLANE:
+        q = plane(dx, dy)
+        send(h_part.at[q], h_in.at[me], 5, dev(core, z, q))
+    g_in[me] = g_part[me]
+    h_in[me] = h_part[me]
+    l_full[core] = mine
+    send(l_full.at[core], l_full.at[core], 4, twin)
+    left(l_in, 0)
     arrived(t_relay.at[0], 15)
     send(t_relay.at[0], t_z.at[low], 3, dev(core, ahead, me))
     arrived(t_relay.at[1], 16)
     send(t_relay.at[1], t_z.at[high], 3, dev(core, behind, me))
     left(t_send.at[low], 15)
     left(t_send.at[high], 16)
-
-    arrived(l_in, 0)
-    mine = (l_chip[core] + (l_in[0] + l_in[1])) * 0.25
-    for cb in range(4):
-        block = dot(mine, total[:, 256 * cb : 256 * cb + 256]) * 0.25
-        for rb in range(4):
-            h_part[4 * rb + cb] = block[8 * rb : 8 * rb + 8]
-    for dx, dy in PLANE:
-        q = plane(dx, dy)
-        send(h_part.at[q], h_in.at[me], 5, dev(core, z, q))
-    h_in[me] = h_part[me]
-
-    packed = dot_t(mine[:16], g_side[0]) + dot_t(mine[16:], g_side[1])
-    for i in range(16):
-        g_part[i] = packed[i : i + 1]
-    for dx, dy in PLANE:
-        q = plane(dx, dy)
-        send(g_part.at[q], g_in.at[me], 6, dev(core, z, q))
-    g_in[me] = g_part[me]
-    l_full[core] = mine
-    send(l_full.at[core], l_full.at[core], 4, twin)
-    left(l_in, 0)
 
     arrived(first(g_in, 15), 6)
     g_sum = added(g_in, 16)
@@ -202,8 +206,8 @@
     h_z[z] = h_sum
     for d in RING:
         send(h_zs, h_z.at[z], 7, dev(core, at_z(d), me))
+    left(first(g_in, 15), 6)
     left(first(h_in, 15), 5)
-    left(first(g_in, 15), 6)
 
     arrived(t_z, 3)
     t_full[mine_t] = (t_send[...] + t_z[...]) * 0.25
@@ -226,10 +230,9 @@
     arrived(first(h_z, 15), 7)
     h_full[slot] = added(h_z, 16)
     for dx, dy in PLANE:
-        send(h_full.at[slot], h_full.at[slot], 11, dev(core, z, plane(dx, dy)), piece_sem.at[me])
-        if hops(dx, dy) > 0:
-            send(h_full.at[slot], h_full.at[slot], 11, dev(other, z, plane(dx, dy)), got.at[12])
-    send(h_full.at[slot], h_full.at[slot], 12, twin)
+        for c in (core, other):
+            send(h_full.at[slot], h_full.at[slot], 11, dev(c, z, plane(dx, dy)))
+    send(h_full.at[slot], h_full.at[slot], 11, twin)
     left(first(h_z, 15), 7)
 
     arrived(t_full.at[other_t], 9)
@@ -257,16 +260,9 @@
     p_out[...] = dot(dot_t(jnp.concatenate([l_full[0], l_full[1]], axis=0).T, inverse), inverse)
     left(first(g_full, 31), 10)
 
-    for dx, dy in reversed(PLANE):
-        q = plane(dx, dy)
-        at = core * 16 + q
-        copies(h_full.at[at], 11, piece_sem.at[q]).wait_recv()
-        if hops(dx, dy) <= 0:
-            send(h_full.at[at], h_full.at[at], 12, twin)
-    left(first(h_full, 15 + FAR), 11)
-    arrived(first(h_full, 16), 12)
+    arrived(first(h_full, 31), 11)
     h_out[...] = h_full[...]
-    left(first(h_full, 16 - FAR), 12)
+    left(first(h_full, 31), 11)
 
 
 def communicate(*args):
@@ -287,7 +283,7 @@
             vmem(12, 8, 512), vmem(6, 8, 512), vmem(6, 8, 512), vmem(2, 3, 8, 512), vmem(6, 8, 512), vmem(12, 8, 512),
             vmem(16, 8, 256), vmem(16, 8, 256), vmem(8, 256), vmem(16, 8, 256), vmem(32, 8, 256),
             vmem(16, 1, 128), vmem(16, 1, 128), vmem(1, 128), vmem(16, 1, 128), vmem(32, 1, 128),
-            dma(11), dma(18), dma(18), dma(16),
+            dma(11), dma(19), dma(19),
         ],
         compiler_params=pltpu.CompilerParams(collective_id=0, has_side_effects=True, vmem_limit_bytes=16 << 20),
     )(*(pltpu.with_memory_space_constraint(v, pltpu.HBM) for v in args))

time: 49.8 us -> 49 us (0.984)
  Pallas kernels: 49 us -> 48.3 us
    pallas_call x1, Pallas kernels: 47.3 us -> 46.6 us  [communicate(): pl.pallas_call(comm_kernel, name='exchange', out_shape=tuple((jax.ShapeDt...]
where the time goes in v4:
time: 49 us; the launch traced here: 48.9 us
  Pallas kernels  48.3 us (99%)
  between operations  0.64 us (1%)
    pallas_call x1, Pallas kernels, communicate(): pl.pallas_call(comm_kernel, name='exchange', out_shape=tuple((jax.ShapeDt...  46.6 us
    pallas_call x1, Pallas kernels, local(): pl.pallas_call(update_kernel, name='update', out_shape=tuple((jax.ShapeDt...  1.67 us

profile of v4, /device:TPU:1, one launch (start us, length us, event | category | flops | bytes accessed | tf_op | source)
XLA Modules:
  0.0 48.9 jit_solution(2045602451890565273)
XLA Ops:
  0.6 46.6 %exchange.1 = (f32[2,8,1024]{2,1,0:T(8,128)S(1)}, f32[2,8,1024]{2,1,0:T(8,128)S(1)}, f32[2,8,2048]{2,1,0:T(8,128)S(1)}, f32[2,8,2048]{2,1,0:T(8,128)S(1)}, f32[1...) custom-call(f32[2,8,1024]{2,1,0:T(8,128)} %sqw.1, ...), custom_call_target="tpu_custom_call" | custom-call | tf_op jit(solution)/shard_map/exchange/pallas_call | solution.py:273
  47.2 1.7 %update.1 = (f32[2,8,1024]{2,1,0:T(8,128)}, f32[2,8,1024]{2,1,0:T(8,128)}, f32[2,8,2048]{2,1,0:T(8,128)}, f32[2,8,2048]{2,1,0:T(8,128)}, f32[128,1024]{1,0:T(8,1...) custom-call(f32[2,8,1024]{2,1,0:T(8,128)S(1)} %get-tuple-element.23.squ, f32[2,8,1024]{2,1,0:T(8,128)S(1)} %get-tuple-element.24.sqv, ...), custom_call_target="tpu_custom_call" | custom-call | tf_op jit(solution)/shard_map/update/pallas_call | solution.py:332

commit v5 on v4

--- a/solution.py
+++ b/solution.py
@@ -145,7 +145,7 @@
     send(corr, corr_in, 2, twin)
     arrived(t_core, 1)
     t_send[...] = term[mine_t] + t_core[...]
-    low, high = pl.ds(0, 3), pl.ds(3, 3)
+    low, high, rest = pl.ds(0, 2), pl.ds(2, 2), pl.ds(4, 2)
     send(t_send.at[low], t_relay.at[0], 15, dev(core, ahead, me))
     send(t_send.at[high], t_relay.at[1], 16, dev(core, behind, me))
     arrived(l_relay.at[0], 13)
@@ -167,7 +167,14 @@
 
     left(l_part.at[0], 13)
     left(l_part.at[1], 14)
+    arrived(t_relay.at[0], 15)
+    send(t_relay.at[0], t_z.at[low], 3, dev(core, ahead, me))
+    arrived(t_relay.at[1], 16)
+    send(t_relay.at[1], t_z.at[high], 3, dev(core, behind, me))
+    left(t_send.at[low], 15)
+    left(t_send.at[high], 16)
     arrived(l_in, 0)
+    send(t_send.at[rest], t_z.at[rest], 18, dev(core, at_z(8), me), got.at[3])
     mine = (l_chip[core] + (l_in[0] + l_in[1])) * 0.25
     packed = dot_t(mine[:16], g_side[0]) + dot_t(mine[16:], g_side[1])
     for i in range(16):
@@ -187,12 +194,6 @@
     l_full[core] = mine
     send(l_full.at[core], l_full.at[core], 4, twin)
     left(l_in, 0)
-    arrived(t_relay.at[0], 15)
-    send(t_relay.at[0], t_z.at[low], 3, dev(core, ahead, me))
-    arrived(t_relay.at[1], 16)
-    send(t_relay.at[1], t_z.at[high], 3, dev(core, behind, me))
-    left(t_send.at[low], 15)
-    left(t_send.at[high], 16)
 
     arrived(first(g_in, 15), 6)
     g_sum = added(g_in, 16)
@@ -212,7 +213,8 @@
     arrived(t_z, 3)
     t_full[mine_t] = (t_send[...] + t_z[...]) * 0.25
     send(t_full.at[mine_t], t_full.at[mine_t], 9, twin)
-    left(t_send, 3)
+    left(t_send.at[pl.ds(0, 4)], 3)
+    left(t_send.at[rest], 18)
     for i in range(8, 11):
         loads[i].wait()
 
@@ -229,8 +231,8 @@
 
     arrived(first(h_z, 15), 7)
     h_full[slot] = added(h_z, 16)
-    for dx, dy in PLANE:
-        for c in (core, other):
+    for c in (core, other):
+        for dx, dy in PLANE:
             send(h_full.at[slot], h_full.at[slot], 11, dev(c, z, plane(dx, dy)))
     send(h_full.at[slot], h_full.at[slot], 11, twin)
     left(first(h_z, 15), 7)
@@ -280,7 +282,7 @@
             vmem(2, 8, 1024), vmem(2, 8, 1024), vmem(2, 8, 2048), vmem(2, 8, 2048), vmem(2, 8, 1024), vmem(2, 8, 2048),
             vmem(128, 1024), vmem(128, 1024), vmem(64, 1024),
             vmem(128, 1024), vmem(2, 32, 128), vmem(2, 32, 128), vmem(2, 32, 128), vmem(2, 32, 128), vmem(2, 32, 128), vmem(2, 32, 128), vmem(2, 128, 128),
-            vmem(12, 8, 512), vmem(6, 8, 512), vmem(6, 8, 512), vmem(2, 3, 8, 512), vmem(6, 8, 512), vmem(12, 8, 512),
+            vmem(12, 8, 512), vmem(6, 8, 512), vmem(6, 8, 512), vmem(2, 2, 8, 512), vmem(6, 8, 512), vmem(12, 8, 512),
             vmem(16, 8, 256), vmem(16, 8, 256), vmem(8, 256), vmem(16, 8, 256), vmem(32, 8, 256),
             vmem(16, 1, 128), vmem(16, 1, 128), vmem(1, 128), vmem(16, 1, 128), vmem(32, 1, 128),
             dma(11), dma(19), dma(19),

time: 49 us -> 48.4 us (0.988)
  Pallas kernels: 48.3 us -> 47.6 us
    pallas_call x1, Pallas kernels: 46.6 us -> 45.9 us  [communicate(): pl.pallas_call(comm_kernel, name='exchange', out_shape=tuple((jax.ShapeDt...]
where the time goes in v5:
time: 48.4 us; the launch traced here: 48.2 us
  Pallas kernels  47.6 us (98%)
  between operations  0.64 us (1%)
    pallas_call x1, Pallas kernels, communicate(): pl.pallas_call(comm_kernel, name='exchange', out_shape=tuple((jax.ShapeDt...  45.9 us
    pallas_call x1, Pallas kernels, local(): pl.pallas_call(update_kernel, name='update', out_shape=tuple((jax.ShapeDt...  1.67 us

profile of v5, /device:TPU:1, one launch (start us, length us, event | category | flops | bytes accessed | tf_op | source)
XLA Modules:
  0.0 48.2 jit_solution(4245511608773025456)
XLA Ops:
  0.6 45.9 %exchange.1 = (f32[2,8,1024]{2,1,0:T(8,128)S(1)}, f32[2,8,1024]{2,1,0:T(8,128)S(1)}, f32[2,8,2048]{2,1,0:T(8,128)S(1)}, f32[2,8,2048]{2,1,0:T(8,128)S(1)}, f32[1...) custom-call(f32[2,8,1024]{2,1,0:T(8,128)} %sqw.1, ...), custom_call_target="tpu_custom_call" | custom-call | tf_op jit(solution)/shard_map/exchange/pallas_call | solution.py:275
  46.6 1.7 %update.1 = (f32[2,8,1024]{2,1,0:T(8,128)}, f32[2,8,1024]{2,1,0:T(8,128)}, f32[2,8,2048]{2,1,0:T(8,128)}, f32[2,8,2048]{2,1,0:T(8,128)}, f32[128,1024]{1,0:T(8,1...) custom-call(f32[2,8,1024]{2,1,0:T(8,128)S(1)} %get-tuple-element.23.squ, f32[2,8,1024]{2,1,0:T(8,128)S(1)} %get-tuple-element.24.sqv, ...), custom_call_target="tpu_custom_call" | custom-call | tf_op jit(solution)/shard_map/update/pallas_call | solution.py:334

commit v6 on v5

--- a/solution.py
+++ b/solution.py
@@ -148,10 +148,28 @@
     low, high, rest = pl.ds(0, 2), pl.ds(2, 2), pl.ds(4, 2)
     send(t_send.at[low], t_relay.at[0], 15, dev(core, ahead, me))
     send(t_send.at[high], t_relay.at[1], 16, dev(core, behind, me))
-    arrived(l_relay.at[0], 13)
-    send(l_relay.at[0], l_in.at[core], 0, dev(0, ahead, me))
-    arrived(l_relay.at[1], 14)
-    send(l_relay.at[1], l_in.at[core], 0, dev(1, behind, me))
+    middle = jnp.logical_and(z >= 4, z < 12)
+
+    def pass_left(way):
+        arrived(l_relay.at[way], 13 + way)
+        send(l_relay.at[way], l_in.at[core], 0, dev(way, (ahead, behind)[way], me))
+
+    def pass_term(way):
+        arrived(t_relay.at[way], 15 + way)
+        send(t_relay.at[way], t_z.at[(low, high)[way]], 3, dev(core, (ahead, behind)[way], me))
+
+    def earlier_first(step):
+        @pl.when(middle)
+        def _():
+            step(0)
+            step(1)
+
+        @pl.when(jnp.logical_not(middle))
+        def _():
+            step(1)
+            step(0)
+
+    earlier_first(pass_left)
     arrived(corr_in, 2)
     total = vec
     total[...] = corr[...] + corr_in[...]
@@ -167,10 +185,7 @@
 
     left(l_part.at[0], 13)
     left(l_part.at[1], 14)
-    arrived(t_relay.at[0], 15)
-    send(t_relay.at[0], t_z.at[low], 3, dev(core, ahead, me))
-    arrived(t_relay.at[1], 16)
-    send(t_relay.at[1], t_z.at[high], 3, dev(core, behind, me))
+    earlier_first(pass_term)
     left(t_send.at[low], 15)
     left(t_send.at[high], 16)
     arrived(l_in, 0)

time: 48.4 us -> 48.1 us (level)
  no operation moved by 1% of the time
where the time goes in v6:
time: 48.1 us; the launch traced here: 47.9 us
  Pallas kernels  47.3 us (98%)
  between operations  0.64 us (1%)
    pallas_call x1, Pallas kernels, communicate(): pl.pallas_call(comm_kernel, name='exchange', out_shape=tuple((jax.ShapeDt...  45.6 us
    pallas_call x1, Pallas kernels, local(): pl.pallas_call(update_kernel, name='update', out_shape=tuple((jax.ShapeDt...  1.67 us

profile of v6, /device:TPU:1, one launch (start us, length us, event | category | flops | bytes accessed | tf_op | source)
XLA Modules:
  0.0 47.9 jit_solution(9121481866865658700)
XLA Ops:
  0.6 45.6 %exchange.1 = (f32[2,8,1024]{2,1,0:T(8,128)S(1)}, f32[2,8,1024]{2,1,0:T(8,128)S(1)}, f32[2,8,2048]{2,1,0:T(8,128)S(1)}, f32[2,8,2048]{2,1,0:T(8,128)S(1)}, f32[1...) custom-call(f32[2,8,1024]{2,1,0:T(8,128)} %sqw.1, ...), custom_call_target="tpu_custom_call" | custom-call | tf_op jit(solution)/shard_map/exchange/pallas_call | solution.py:290
  46.3 1.7 %update.1 = (f32[2,8,1024]{2,1,0:T(8,128)}, f32[2,8,1024]{2,1,0:T(8,128)}, f32[2,8,2048]{2,1,0:T(8,128)}, f32[2,8,2048]{2,1,0:T(8,128)}, f32[128,1024]{1,0:T(8,1...) custom-call(f32[2,8,1024]{2,1,0:T(8,128)S(1)} %get-tuple-element.23.squ, f32[2,8,1024]{2,1,0:T(8,128)S(1)} %get-tuple-element.24.sqv, ...), custom_call_target="tpu_custom_call" | custom-call | tf_op jit(solution)/shard_map/update/pallas_call | solution.py:349
